TPU v7x, 32 devices: a whole 2x2x4 slice. The times are simulated.
32 devices in a mesh: tok: 16 (over z, x, core), head: 2 (over y).
Axes of the slice: x: 2, y: 2, z: 4, core: 2. Of those that a mesh axis runs over, the one named last changes fastest.
Arguments:
- queries: bfloat16 [1024, 4096], P('tok', 'head'), may hold values from -6 to 6
- keys: bfloat16 [8192, 1024], P('tok', 'head'), may hold values from -256 to 256
- values: bfloat16 [8192, 1024], P('tok', 'head'), may hold values from -6 to 6
- out_weight: bfloat16 [4096, 4096], P('head'), may hold values from -0.59765625 to 0.59765625
- task_slot: int32 [8, 8, 16], P('head'), may hold values from -1 to 7, as said below
- task_count: int32 [8, 16], P('head'), may hold values from 1 to 8, as said below
Outputs:
- projected: bfloat16 [1024, 4096], P('tok', 'head')
Inputs may be any that keep to these rules, and one draw needn't show every extreme that they name: For each key head h and key block c, the entries task_slot[h, b, c] that are not -1 take each of the values 0 to task_count[h, c] - 1 exactly once. Key blocks 0 and 15 are attended by every query block under every key head. task_count[h, c] is the number of query blocks that attend key block c under key head h.
All inputs are finite; a program needn't handle non-finite values.
Results may differ from a plain program's by a relative error of at most 0.015.
Values may be sent and summed in bfloat16 or wider, within the bound.
No kernel may reach another device: no remote copies, remote signals or barrier semaphores. Data moves between devices by JAX's collectives and lax.ppermute only.
A program may use at most 64 MiB of HBM per device.

v0:
```python
import jax
import jax.numpy as jnp
from jax import lax
from jax.sharding import PartitionSpec as P

HEADS = 32
KVH = 8
HEAD_SIZE = 128
QBLK = 128
theta_base = 500000.0
neg_fill = -1e30


def rotate(block_rows, first_row):
    head_width = block_rows.shape[-1]
    half_width = head_width // 2
    frequency = theta_base ** (-(jnp.arange(half_width, dtype=jnp.float32) * (2.0 / head_width)))
    places = (first_row + jnp.arange(block_rows.shape[0], dtype=jnp.int32)).astype(jnp.float32)
    angles = places[:, None] * frequency[None, :]
    cosine = jnp.cos(angles)[:, None, :]
    sine_table = jnp.sin(angles)[:, None, :]
    first_half = block_rows[..., :half_width]
    second_half = block_rows[..., half_width:]
    return jnp.concatenate(
        [
            first_half * cosine - second_half * sine_table,
            second_half * cosine + first_half * sine_table,
        ],
        axis=-1,
    )


def block_partial(query_row_block, head_keys_matrix, head_values_matrix):
    attention_logits = jnp.einsum(
        "qgd,kd->gqk", query_row_block, head_keys_matrix, preferred_element_type=jnp.float32
    ) * HEAD_SIZE ** (-0.5)
    maxima = jnp.max(attention_logits, axis=-1)
    probabilities = jnp.exp(attention_logits - maxima[..., None])
    totals = jnp.sum(probabilities, axis=-1)
    weighted_value_sum = jnp.einsum(
        "gqk,kd->qgd",
        probabilities.astype(jnp.bfloat16),
        head_values_matrix,
        preferred_element_type=jnp.float32,
    )
    normed = (weighted_value_sum / jnp.transpose(totals)[:, :, None]).astype(jnp.bfloat16)
    logsum = jnp.transpose(maxima + jnp.log(totals))
    return (normed, logsum)


def place_rows(buffers, cand_index, kv_local, row_start, normed, logsum):
    normed_all, logsum_all = buffers
    head_span = normed.shape[1]
    group_size = logsum.shape[1]
    column_normed = kv_local * head_span
    column_logsum = kv_local * group_size
    fresh_normed = normed[None]
    fresh_logsum = logsum[None]
    normed_all = lax.dynamic_update_slice(
        normed_all, fresh_normed, (cand_index, row_start, column_normed)
    )
    logsum_all = lax.dynamic_update_slice(
        logsum_all, fresh_logsum, (cand_index, row_start, column_logsum)
    )
    return (normed_all, logsum_all)


def column_at(task_slot, kv_local, server):
    return lax.dynamic_index_in_dim(task_slot[kv_local], server, 1, keepdims=False)


def count_at(task_count, kv_local, server):
    return lax.dynamic_index_in_dim(task_count[kv_local], server, 0, keepdims=False)


def run_slots(buffers, gathered, plan_entry, kv_local, group_size, blocks):
    cand_index, head_keys_matrix, head_values_matrix, column, range_low, range_high = plan_entry
    head_span = group_size * HEAD_SIZE
    block_ids = jnp.arange(blocks, dtype=jnp.int32)
    matches = column[:, None] == block_ids[None, :]
    lookup = jnp.sum(jnp.where(matches, block_ids[:, None], 0), axis=0)

    def step(slot_index, current):
        row_start = lookup[slot_index] * QBLK
        query_row_block = lax.dynamic_slice(
            gathered, (row_start, kv_local * head_span), (QBLK, head_span)
        ).reshape(QBLK, group_size, HEAD_SIZE)
        normed, logsum = block_partial(query_row_block, head_keys_matrix, head_values_matrix)
        return place_rows(
            current, cand_index, kv_local, row_start, normed.reshape(QBLK, head_span), logsum
        )

    return lax.fori_loop(range_low, range_high, step, buffers)


def on_device(queries, keys, values, out_weight, task_slot, task_count):
    servers = lax.axis_size("tok")
    server_index = lax.axis_index("tok")
    rows_dev = queries.shape[0]
    local_kv = task_slot.shape[0]
    blocks = task_slot.shape[1]
    group_size = HEADS // KVH
    head_span = group_size * HEAD_SIZE
    total_rows = rows_dev * servers
    shaped = queries.astype(jnp.float32).reshape(rows_dev, local_kv * group_size, HEAD_SIZE)
    rotated = (
        rotate(shaped, server_index * rows_dev)
        .astype(jnp.bfloat16)
        .reshape(rows_dev, local_kv * head_span)
    )
    task_plans = []
    for kv_local in range(local_kv):
        task_plans.append(
            [
                (
                    0,
                    keys[:, kv_local * HEAD_SIZE : (kv_local + 1) * HEAD_SIZE],
                    values[:, kv_local * HEAD_SIZE : (kv_local + 1) * HEAD_SIZE],
                    column_at(task_slot, kv_local, server_index),
                    jnp.int32(0),
                    count_at(task_count, kv_local, server_index),
                )
            ]
        )
    cand_total = 1
    initial = (
        jnp.zeros((cand_total, total_rows, local_kv * head_span), jnp.bfloat16),
        jnp.full((cand_total, total_rows, local_kv * group_size), neg_fill, jnp.float32),
    )
    gathered = lax.all_gather(rotated, "tok", axis=0, tiled=True)
    buffers = initial
    for kv_local in range(local_kv):
        for plan_entry in task_plans[kv_local]:
            buffers = run_slots(buffers, gathered, plan_entry, kv_local, group_size, blocks)
    normed_all, logsum_all = buffers
    back_normed = lax.all_to_all(normed_all[None], "tok", split_axis=2, concat_axis=0, tiled=True)
    back_logsum = lax.all_to_all(logsum_all[None], "tok", split_axis=2, concat_axis=0, tiled=True)
    sources = back_logsum.shape[0] * back_logsum.shape[1]
    logsum_recv = back_logsum.reshape(sources, rows_dev, local_kv * group_size)
    normed_recv = back_normed.reshape(sources, rows_dev, local_kv * group_size, HEAD_SIZE)
    largest = jnp.max(logsum_recv, axis=0)
    weights = jnp.exp(logsum_recv - largest[None])
    numerator = jnp.einsum("sqh,sqhd->qhd", weights, normed_recv.astype(jnp.float32))
    attention = (
        (numerator / jnp.sum(weights, axis=0)[:, :, None])
        .astype(jnp.bfloat16)
        .reshape(rows_dev, local_kv * head_span)
    )
    partial_out = jnp.dot(attention, out_weight, preferred_element_type=jnp.float32)
    return lax.psum_scatter(
        partial_out.astype(jnp.bfloat16), "head", scatter_dimension=1, tiled=True
    )


def solution(mesh):
    placed = (
        P("tok", "head"),
        P("tok", "head"),
        P("tok", "head"),
        P("head", None),
        P("head", None, None),
        P("head", None),
    )
    return jax.shard_map(
        on_device, mesh=mesh, in_specs=placed, out_specs=P("tok", "head"), check_vma=False
    )
```

profile of v0, /device:TPU:0, one launch (start us, length us, event | category | flops | bytes accessed | tf_op | source)
XLA Modules:
  0.0 463.4 jit_solution(422942893577546123)
XLA Ops:
  6.6 1.1 convert_bitcast_fusion
  11.9 50.7 %all-gather.2.cloned.1.call-done = bf16[1024,2048]{1,0:T(8,128)(2,1)} async-done(((bf16[64,2048]{1,0:T(8,128)(2,1)}), bf16[1024,2048]{1,0:T(8,128)(2,1)}) %all-gather.2.cloned.1.call-update) | async-done | bytes 4194320 | tf_op jit(solution)/shard_map/all_gather | solution.py:130
  62.7 6.4 %copy.78 = bf16[1024,2048]{0,1:T(8,128)(2,1)} copy(bf16[1024,2048]{1,0:T(8,128)(2,1)} %all-gather.2.cloned.1.call-done) | data formatting | bytes 8388608 | tf_op jit(solution)/shard_map/while | solution.py:93
  69.1 2.5 broadcast_in_dim.80
  71.5 38.5 %while.48 = (s32[]{:T(128)}, bf16[1,1024,2048]{1,2,0:T(8,128)(2,1)}, f32[1,1024,16]{1,2,0:T(8,128)S(1)}, s32[]{:T(128)}, s32[8]{0:T(128)S(1)}, /*index=5*/bf16[1...) while((s32[]{:T(128)}, ...), condition=%wide.region_4.5_spmd, body=%wide.region_1.4_spmd.sunk | while | flops 135921152 | bytes 4210925 | solution.py:93
  82.9 0.9 constant_dynamic-slice_fusion.12
  92.3 0.9 constant_dynamic-slice_fusion.12
  110.0 38.9 %while.49 = (s32[]{:T(128)}, bf16[1,1024,2048]{1,2,0:T(8,128)(2,1)}, f32[1,1024,16]{1,2,0:T(8,128)S(1)}, s32[]{:T(128)}, s32[8]{0:T(128)S(1)}, /*index=5*/bf16[1...) while((s32[]{:T(128)}, ...), condition=%wide.region_9.10_spmd, body=%wide.region_6.9_spmd.sunk | while | flops 135921152 | bytes 4210925 | solution.py:93
  149.0 38.4 %while.50 = (s32[]{:T(128)}, bf16[1,1024,2048]{1,2,0:T(8,128)(2,1)}, f32[1,1024,16]{1,2,0:T(8,128)S(1)}, s32[]{:T(128)}, s32[8]{0:T(128)S(1)}, /*index=5*/bf16[1...) while((s32[]{:T(128)}, ...), condition=%wide.region_14.15_spmd, body=%wide.region_11.14_spmd.sunk | while | flops 135921152 | bytes 4210925 | solution.py:93
  187.4 38.3 %while.51 = (s32[]{:T(128)}, bf16[1,1024,2048]{1,2,0:T(8,128)(2,1)}, f32[1,1024,16]{1,2,0:T(8,128)S(1)}, s32[]{:T(128)}, s32[8]{0:T(128)S(1)}, /*index=5*/bf16[1...) while((s32[]{:T(128)}, ...), condition=%wide.region_19.20_spmd, body=%wide.region_16.19_spmd.sunk | while | flops 135921152 | bytes 4210925 | solution.py:93
  226.5 2.0 reduce.10
  229.3 3.5 all-to-all-start
  232.8 20.7 %copy.89 = bf16[1,1,1024,2048]{3,1,0,2:T(2,128)(2,1)} copy(bf16[1,1,1024,2048]{2,3,1,0:T(8,128)(2,1)} %bitcast.233) | data formatting | bytes 8388608 | tf_op jit(solution)/shard_map/broadcast_in_dim | solution.py:136
  254.1 26.7 %reduce.12 = bf16[1024,2048]{1,0:T(8,128)(2,1)} reduce(bf16[1024,1,1,2048]{3,2,1,0:T(2,128)(2,1)} %bitcast.232, bf16[]{:T(256)} %broadcast.91), dimensions={1,2}, to_apply=%bitcast.126.reduce_sub_computation | reduce | bytes 8388610
  280.8 11.4 %reshape.171 = bf16[16,2,65536]{2,1,0:T(2,128)(2,1)} reshape(bf16[1024,2048]{1,0:T(8,128)(2,1)} %reduce.12) | data formatting | bytes 8388608
  292.2 6.0 %all-to-all-start.1 = ((bf16[16,2,65536]{2,1,0:T(2,128)(2,1)}), bf16[16,2,65536]{2,1,0:T(2,128)(2,1)}, u32[]{:S(2)}, u32[]{:S(2)}) async-start(bf16[16,2,65536]{2,1,0:T(2,128)(2,1)} %reshape.171), calls=%async_computation.1 | async-start | bytes 8388608 | tf_op jit(solution)/shard_map/all_to_all | solution.py:136
  299.3 0.9 reshape.170
  301.3 74.5 %all-to-all-done.1 = bf16[16,2,65536]{2,1,0:T(2,128)(2,1)} async-done(((bf16[16,2,65536]{2,1,0:T(2,128)(2,1)}), bf16[16,2,65536]{2,1,0:T(2,128)(2,1)}, u32[]{:S(2)}, u32[]{:S(2)}) %all-to-all-start.1) | async-done | bytes 4194336 | tf_op jit(solution)/shard_map/all_to_all | solution.py:136
  375.8 12.3 %reshape.172 = bf16[1024,1,1,2048]{3,2,1,0:T(2,128)(2,1)} reshape(bf16[16,2,65536]{2,1,0:T(2,128)(2,1)} %all-to-all-done.1) | data formatting | bytes 8388608
  388.1 24.7 %bitcast_reduce_fusion = bf16[1024,2048]{1,0:T(8,128)(2,1)S(1)} fusion(bf16[1024,1,1,2048]{3,2,1,0:T(2,128)(2,1)} %reshape.172), kind=kLoop, calls=%fused_computation.102 | loop fusion | bytes 8388608 | tf_op jit(solution)/shard_map/all_to_all | solution.py:136
  412.8 1.4 copy.106
  414.2 2.8 fusion.36
  417.2 9.6 %convolution_convert_fusion = bf16[64,4096]{1,0:T(8,128)(2,1)} fusion(bf16[2048,4096]{1,0:T(8,128)(2,1)} %param.17, bf16[8,8,16,128]{3,2,1,0:T(8,128)(2,1)S(1)} %bitcast.248), kind=kOutput, calls=%fused_computation.60 | convolution fusion | flops 1074003968 | bytes 17563648 | tf_op jit(solution)/shard_map/dot_general | solution.py:149
  426.8 29.8 %reduce-scatter.2.cloned.1.call-done = bf16[64,2048]{1,0:T(8,128)(2,1)} async-done(((bf16[64,4096]{1,0:T(8,128)(2,1)}), bf16[64,2048]{1,0:T(8,128)(2,1)}) %reduce-scatter.2.cloned.1.call-update) | async-done | bytes 262160 | tf_op jit(solution)/shard_map/reduce_scatter | solution.py:150
  (272 shorter events, 115.9 us)
Async XLA Ops:
  6.5 2.6 copy-start
  6.5 3.2 copy-start.3
  6.5 4.5 copy-start.2
  6.5 5.3 %copy-start.1 = (bf16[512,512]{1,0:T(8,128)(2,1)S(1)}, bf16[512,512]{1,0:T(8,128)(2,1)}, u32[]{:S(2)}) copy-start(bf16[512,512]{1,0:T(8,128)(2,1)} %param.15) | copy-start | bytes 1572868
  6.5 56.1 %all-gather.2.cloned.1.call-start = ((), (), s32[]{:S(2)}) async-start(), calls=%async_computation.3 | async-start | bytes 4456448 | tf_op jit(solution)/shard_map/all_gather | solution.py:130
  229.3 62.9 %all-to-all-start = ((f32[16,1,1024]{2,1,0:T(1,128)}), f32[16,1,1024]{2,1,0:T(1,128)S(1)}, u32[]{:S(2)}, u32[]{:S(2)}) async-start(f32[16,1,1024]{2,1,0:T(1,128)} %reshape.169), calls=%async_computation | async-start | bytes 131072 | tf_op jit(solution)/shard_map/all_to_all | solution.py:137
  292.2 83.6 %all-to-all-start.1 = ((bf16[16,2,65536]{2,1,0:T(2,128)(2,1)}), bf16[16,2,65536]{2,1,0:T(2,128)(2,1)}, u32[]{:S(2)}, u32[]{:S(2)}) async-start(bf16[16,2,65536]{2,1,0:T(2,128)(2,1)} %reshape.171), calls=%async_computation.1 | async-start | bytes 8388608 | tf_op jit(solution)/shard_map/all_to_all | solution.py:136
  298.2 158.3 %reduce-scatter.2.cloned.1.call-start = ((), (), s32[]{:S(2)}) async-start(), calls=%async_computation.4 | async-start | bytes 786432 | tf_op jit(solution)/shard_map/reduce_scatter | solution.py:150
Sparse Core Ops, SparseCore 0:
  9.5 53.0 all-gather.1
  426.9 29.5 reduce-scatter.1
where the time goes:
time: 466 us; the launch traced here: 463 us
  local copies, waits for them, and re-layouts  157 us (34%)
  waiting for transfers between devices  155 us (33%)
  loops' own time  45 us (10%)
  other arithmetic  43.2 us (9%)
  matrix products  39.9 us (9%)
  between operations  13.7 us (3%)
  starting transfers between devices  9.78 us (2%)
    all_to_all x1, waiting for transfers between devices, on_device(): lax.all_to_all(normed_all[None], 'tok', split_axis=2, concat_axis=0, tile...  74.5 us
    all_gather x1, waiting for transfers between devices, on_device(): gathered = lax.all_gather(rotated, 'tok', axis=0, tiled=True)  50.7 us
    another operation x4, loops' own time, run_slots(): return lax.fori_loop(range_low, range_high, step, buffers)  45 us
    unnamed x3, other arithmetic  29.8 us
    reduce_scatter x1, waiting for transfers between devices, on_device(): lax.psum_scatter(partial_out.astype(jnp.bfloat16), 'head', scatter_dimens...  29.8 us
    unnamed x21, local copies, waits for them, and re-layouts  29.4 us
    dynamic_slice x32, local copies, waits for them, and re-layouts, step(): lax.dynamic_slice(gathered, (row_start, kv_local * head_span), (QBLK, hea...  29.4 us
    all_to_all x1, local copies, waits for them, and re-layouts, on_device(): lax.all_to_all(normed_all[None], 'tok', split_axis=2, concat_axis=0, tile...  24.7 us
  transfers between devices with their start and end apart: 4, of which 3 were waited for; matrix products, arithmetic and copies ran while one was open for 14% of the time, Pallas kernels for 0%

commit v1 on v0

--- a/solution.py
+++ b/solution.py
@@ -133,7 +133,12 @@
         for plan_entry in task_plans[kv_local]:
             buffers = run_slots(buffers, gathered, plan_entry, kv_local, group_size, blocks)
     normed_all, logsum_all = buffers
-    back_normed = lax.all_to_all(normed_all[None], "tok", split_axis=2, concat_axis=0, tiled=True)
+    back_normed = jnp.concatenate(
+        lax.all_to_all(
+            jnp.stack(jnp.split(normed_all[None], lax.axis_size("tok"), axis=2)), "tok", 0, 0
+        ),
+        axis=0,
+    )
     back_logsum = lax.all_to_all(logsum_all[None], "tok", split_axis=2, concat_axis=0, tiled=True)
     sources = back_logsum.shape[0] * back_logsum.shape[1]
     logsum_recv = back_logsum.reshape(sources, rows_dev, local_kv * group_size)

time: 466 us -> 395 us (0.85)
  local copies, waits for them, and re-layouts: 157 us -> 115 us
  other arithmetic: 43.2 us -> 16.2 us
    unnamed x3 -> x2, other arithmetic: 29.8 us -> 2.93 us
    all_to_all x1 -> x0, local copies, waits for them, and re-layouts: 24.7 us -> none  [on_device(): lax.all_to_all(normed_all[None], 'tok', split_axis=2, concat_axis=0, tile...]
    broadcast_in_dim x1 -> x0, local copies, waits for them, and re-layouts: 20.7 us -> none  [on_device(): normed_all[None]]
    while x2 -> x3, local copies, waits for them, and re-layouts: 6.6 us -> 13.1 us  [run_slots(): return lax.fori_loop(range_low, range_high, step, buffers)]
    unnamed x21 -> x35, local copies, waits for them, and re-layouts: 29.4 us -> 25.8 us
  transfers between devices with their start and end apart: 4 -> 4, of which waited for: 3 -> 3; matrix products, arithmetic and copies ran while one was open for 14% -> 8% of each run, Pallas kernels for 0% -> 0%
where the time goes in v1:
time: 395 us; the launch traced here: 393 us
  waiting for transfers between devices  155 us (39%)
  local copies, waits for them, and re-layouts  115 us (29%)
  loops' own time  43 us (11%)
  matrix products  39.9 us (10%)
  other arithmetic  16.2 us (4%)
  between operations  13.7 us (3%)
  starting transfers between devices  9.78 us (2%)
    all_to_all x1, waiting for transfers between devices, on_device(): lax.all_to_all(jnp.stack(jnp.split(normed_all[None], lax.axis_size('tok')...  74.6 us
    all_gather x1, waiting for transfers between devices, on_device(): gathered = lax.all_gather(rotated, 'tok', axis=0, tiled=True)  50.7 us
    another operation x4, loops' own time, run_slots(): return lax.fori_loop(range_low, range_high, step, buffers)  43 us
    reduce_scatter x1, waiting for transfers between devices, on_device(): lax.psum_scatter(partial_out.astype(jnp.bfloat16), 'head', scatter_dimens...  29.8 us
    dynamic_slice x32, local copies, waits for them, and re-layouts, step(): lax.dynamic_slice(gathered, (row_start, kv_local * head_span), (QBLK, hea...  29.4 us
    unnamed x35, local copies, waits for them, and re-layouts  25.8 us
    dynamic_update_slice x32, local copies, waits for them, and re-layouts, place_rows(): lax.dynamic_update_slice(normed_all, fresh_normed, (cand_index, row_start...  22 us
    dynamic_slice x32, local copies, waits for them, and re-layouts, step(): row_start = lookup[slot_index] * QBLK  18.8 us
  transfers between devices with their start and end apart: 4, of which 3 were waited for; matrix products, arithmetic and copies ran while one was open for 8% of the time, Pallas kernels for 0%

profile of v1, /device:TPU:0, one launch (start us, length us, event | category | flops | bytes accessed | tf_op | source)
XLA Modules:
  0.0 392.8 jit_solution(11951555893118960728)
XLA Ops:
  11.9 50.7 %all-gather.2.cloned.1.call-done = bf16[1024,2048]{1,0:T(8,128)(2,1)} async-done(((bf16[64,2048]{1,0:T(8,128)(2,1)}), bf16[1024,2048]{1,0:T(8,128)(2,1)}) %all-gather.2.cloned.1.call-update) | async-done | bytes 4194320 | tf_op jit(solution)/shard_map/all_gather | solution.py:130
  62.6 6.4 %copy.59 = bf16[1024,2048]{0,1:T(8,128)(2,1)} copy(bf16[1024,2048]{1,0:T(8,128)(2,1)} %all-gather.2.cloned.1.call-done) | data formatting | bytes 8388608 | tf_op jit(solution)/shard_map/while | solution.py:93
  69.0 2.5 broadcast_in_dim.80
  71.5 38.4 %while.48 = (s32[]{:T(128)}, bf16[1,1024,2048]{1,2,0:T(8,128)(2,1)}, f32[1,1024,16]{1,2,0:T(8,128)S(1)}, s32[]{:T(128)}, s32[8]{0:T(128)S(1)}, /*index=5*/bf16[1...) while((s32[]{:T(128)}, ...), condition=%wide.region_4.5_spmd, body=%wide.region_1.4_spmd.sunk | while | flops 135921152 | bytes 4210925 | solution.py:93
  109.9 37.8 %while.49 = (s32[]{:T(128)}, bf16[1,1024,2048]{1,2,0:T(8,128)(2,1)}, f32[1,1024,16]{1,2,0:T(8,128)S(1)}, s32[]{:T(128)}, s32[8]{0:T(128)S(1)}, /*index=5*/bf16[1...) while((s32[]{:T(128)}, ...), condition=%wide.region_9.10_spmd, body=%wide.region_6.9_spmd.sunk | while | flops 135921152 | bytes 4210925 | solution.py:93
  147.7 38.0 %while.50 = (s32[]{:T(128)}, bf16[1,1024,2048]{1,2,0:T(8,128)(2,1)}, f32[1,1024,16]{1,2,0:T(8,128)S(1)}, s32[]{:T(128)}, s32[8]{0:T(128)S(1)}, /*index=5*/bf16[1...) while((s32[]{:T(128)}, ...), condition=%wide.region_14.15_spmd, body=%wide.region_11.14_spmd.sunk | while | flops 135921152 | bytes 4210925 | solution.py:93
  185.7 37.9 %while.51 = (s32[]{:T(128)}, bf16[1,1024,2048]{1,2,0:T(8,128)(2,1)}, f32[1,1024,16]{1,2,0:T(8,128)S(1)}, s32[]{:T(128)}, s32[8]{0:T(128)S(1)}, /*index=5*/bf16[1...) while((s32[]{:T(128)}, ...), condition=%wide.region_19.20_spmd, body=%wide.region_16.19_spmd.sunk | while | flops 135921152 | bytes 4210925 | solution.py:93
  224.4 1.9 reduce.8
  227.1 3.5 all-to-all-start
  230.6 6.5 %copy.69 = bf16[1,1024,2048]{2,1,0:T(8,128)(2,1)} copy(bf16[1,1024,2048]{1,2,0:T(8,128)(2,1)} %get-tuple-element.188) | data formatting | bytes 8388608 | tf_op jit(solution)/shard_map/while | solution.py:93
  237.1 1.8 fusion.55
  238.9 1.7 fusion.54
  240.6 1.7 fusion.53
  242.3 1.7 fusion.52
  244.0 1.7 fusion.51
  245.6 1.7 fusion.50
  247.3 1.7 fusion.49
  249.0 1.7 fusion.48
  256.5 6.0 %all-to-all-start.1 = ((bf16[16,1,1,64,2048]{4,3,2,1,0:T(8,128)(2,1)}), bf16[16,1,1,64,2048]{4,3,2,1,0:T(8,128)(2,1)}, u32[]{:S(2)}, u32[]{:S(2)}) async-start(bf16[16,1,1,64,2048]{4,3,2,1,0:T(8,128)(2,1)} %fusion.40), calls=%async_computation.1 | async-start | bytes 8388608 | tf_op jit(solution)/shard_map/all_to_all | solution.py:137
  265.4 74.6 %all-to-all-done.1 = bf16[16,1,1,64,2048]{4,3,2,1,0:T(8,128)(2,1)} async-done(((bf16[16,1,1,64,2048]{4,3,2,1,0:T(8,128)(2,1)}), bf16[16,1,1,64,2048]{4,3,2,1,0:T(8,128)(2,1)}, u32[]{:S(2)}, u32[]{:S(2)}) %all-to-all-start.1) | async-done | bytes 4194336 | tf_op jit(solution)/shard_map/all_to_all | solution.py:137
  340.0 3.6 copy.84
  343.6 2.8 fusion.36
  346.6 9.6 %convolution_convert_fusion = bf16[64,4096]{1,0:T(8,128)(2,1)} fusion(bf16[2048,4096]{1,0:T(8,128)(2,1)} %param.17, bf16[8,8,16,128]{3,2,1,0:T(8,128)(2,1)S(1)} %bitcast.324), kind=kOutput, calls=%fused_computation.60 | convolution fusion | flops 1074003968 | bytes 17563648 | tf_op jit(solution)/shard_map/dot_general | solution.py:154
  356.3 29.8 %reduce-scatter.2.cloned.1.call-done = bf16[64,2048]{1,0:T(8,128)(2,1)} async-done(((bf16[64,4096]{1,0:T(8,128)(2,1)}), bf16[64,2048]{1,0:T(8,128)(2,1)}) %reduce-scatter.2.cloned.1.call-update) | async-done | bytes 262160 | tf_op jit(solution)/shard_map/reduce_scatter | solution.py:155
  (285 shorter events, 124.8 us)
Async XLA Ops:
  6.5 2.6 copy-start.1
  6.5 3.2 copy-start.4
  6.5 4.5 %copy-start.3 = (s32[4,8,16]{2,1,0:T(8,128)S(1)}, s32[4,8,16]{2,1,0:T(8,128)}, u32[]{:S(2)}) copy-start(s32[4,8,16]{2,1,0:T(8,128)} %param.18) | copy-start | bytes 6148
  6.5 5.3 %copy-start.2 = (bf16[512,512]{1,0:T(8,128)(2,1)S(1)}, bf16[512,512]{1,0:T(8,128)(2,1)}, u32[]{:S(2)}) copy-start(bf16[512,512]{1,0:T(8,128)(2,1)} %param.15) | copy-start | bytes 1572868
  6.5 56.1 %all-gather.2.cloned.1.call-start = ((), (), s32[]{:S(2)}) async-start(), calls=%async_computation.3 | async-start | bytes 4456448 | tf_op jit(solution)/shard_map/all_gather | solution.py:130
  227.1 29.4 %all-to-all-start = ((f32[16,1,1024]{2,1,0:T(1,128)}), f32[16,1,1024]{2,1,0:T(1,128)S(1)}, u32[]{:S(2)}, u32[]{:S(2)}) async-start(f32[16,1,1024]{2,1,0:T(1,128)} %reshape.160), calls=%async_computation | async-start | bytes 131072 | tf_op jit(solution)/shard_map/all_to_all | solution.py:142
  237.1 13.5 %copy-start = (bf16[1,1024,2048]{2,1,0:T(8,128)(2,1)S(1)}, bf16[1,1024,2048]{2,1,0:T(8,128)(2,1)}, u32[]{:S(2)}) copy-start(bf16[1,1024,2048]{2,1,0:T(8,128)(2,1)} %copy.69) | copy-start | bytes 12582916
  256.5 83.6 %all-to-all-start.1 = ((bf16[16,1,1,64,2048]{4,3,2,1,0:T(8,128)(2,1)}), bf16[16,1,1,64,2048]{4,3,2,1,0:T(8,128)(2,1)}, u32[]{:S(2)}, u32[]{:S(2)}) async-start(bf16[16,1,1,64,2048]{4,3,2,1,0:T(8,128)(2,1)} %fusion.40), calls=%async_computation.1 | async-start | bytes 8388608 | tf_op jit(solution)/shard_map/all_to_all | solution.py:137
  262.5 123.5 %reduce-scatter.2.cloned.1.call-start = ((), (), s32[]{:S(2)}) async-start(), calls=%async_computation.4 | async-start | bytes 786432 | tf_op jit(solution)/shard_map/reduce_scatter | solution.py:155
Sparse Core Ops, SparseCore 0:
  9.5 53.0 all-gather.1
  356.4 29.5 reduce-scatter.1
